TPU v7x, 32 devices: a whole 2x2x4 slice. The times are simulated.
32 devices in a mesh: groups: 2 (over y), seq: 4 (over z), inner: 2 (over x), head: 2 (over core).
Axes of the slice: x: 2, y: 2, z: 4, core: 2. Of those that a mesh axis runs over, the one named last changes fastest.
Arguments:
- queries: bfloat16 [2048, 32, 128], P(('groups', 'seq', 'inner'), 'head'), parts along dimension 0, as said below
- keys: bfloat16 [2048, 4, 128], P(('groups', 'seq', 'inner'), 'head'), parts along dimension 0
- values: bfloat16 [2048, 4, 128], P(('groups', 'seq', 'inner'), 'head'), parts along dimension 0, may hold values from -6 to 6
- log_decay: float32 [2048, 4], P(('groups', 'seq', 'inner'), 'head'), parts along dimension 0, as said below
- gain: float32 [32, 128], P('head'), may hold values from 0.1 to 1.9
- block_list: int32 [32, 16], P(('groups', 'seq', 'inner')), parts along dimension 0, may hold values from 0 to 15, as said below
Outputs:
- attended: bfloat16 [2048, 32, 128], P(('groups', 'seq', 'inner'), 'head'), parts along dimension 0
There are 2 independent parts, one for each index of `groups`. A program takes and returns all parts, laid end to end along the dimension named above; an argument that names none is the same for every part. Nothing has to cross between parts.
Inputs may be any that keep to these rules, and one draw needn't show every extreme that they name: Keys lie within -6 to 6; queries within -144 to 144. `log_decay`: each entry is below 0. `block_list`: entry 0 of row b is b. The sequence's pieces of 128 tokens fall into segments: piece p belongs to segment p modulo 2. Every entry of row b is a block at or before b in a piece of b's segment.
All inputs are finite; a program needn't handle non-finite values.
Results may differ from a plain program's by a relative error of at most 0.0017.
Values may be sent and summed in bfloat16 or wider, within the bound.
A program may use at most 64 MiB of HBM per device.

v0:
```python
import jax
import jax.numpy as jnp
from jax import lax
from jax.sharding import PartitionSpec as P

BLK = 64
SEL = 16
HIGH = lax.Precision.HIGHEST


def prefix(shard, axis, combine, identity):
    devices, here = (lax.axis_size(axis), lax.axis_index(axis))
    everything = jax.tree.map(lambda part: lax.all_gather(part, axis), shard)
    start = jax.tree.map(
        lambda part, zero: jnp.broadcast_to(jnp.asarray(zero, part.dtype), part.shape),
        shard,
        identity,
    )

    def turn(k, before):
        reached = k < here
        new = combine(before, jax.tree.map(lambda part: part[k], everything))
        return jax.tree.map(lambda a, b: jnp.where(reached, a, b), new, before)

    return lax.fori_loop(0, devices, turn, start)


def combine(earlier, later):
    return (earlier[0] * later[0], later[0][:, None, None] * earlier[1] + later[1])


def shards(queries, keys, values, log_decay, gain, block_list):
    tokens, heads_loc, width = queries.shape
    kv_loc = keys.shape[1]
    rep = heads_loc // kv_loc
    qf = queries.astype(jnp.float32).reshape(tokens, kv_loc, rep, width)
    kf = keys.astype(jnp.float32)
    vf = values.astype(jnp.float32)
    cum = jnp.cumsum(log_decay, axis=0)
    total = cum[-1]
    causal = jnp.arange(tokens)[:, None] >= jnp.arange(tokens)[None, :]
    scores = jnp.einsum("tkrd,skd->krts", qf, kf, precision=HIGH)
    diff = cum.T[:, :, None] - cum.T[:, None, :]
    weight = jnp.where(causal[None], jnp.exp(jnp.minimum(diff, 0.0)), 0.0)
    intra = jnp.einsum("krts,skd->tkrd", scores * weight[:, None], vf, precision=HIGH)
    tail = jnp.exp(total[None, :] - cum)
    own_state = jnp.einsum("skd,ske->kde", kf * tail[:, :, None], vf, precision=HIGH)
    own_decay = jnp.exp(total)
    identity = (jnp.ones_like(own_decay), jnp.zeros_like(own_state))
    prior = prefix((own_decay, own_state), ("seq", "inner"), combine, identity)
    prior_state = prior[1]
    inter = jnp.exp(cum)[:, :, None, None] * jnp.einsum(
        "tkrd,kde->tkre", qf, prior_state, precision=HIGH
    )
    linear = (intra + inter).reshape(tokens, heads_loc, width)
    normed = (
        linear * lax.rsqrt(jnp.mean(linear * linear, axis=-1, keepdims=True) + 1e-06) * gain[None]
    )
    per_piece = tokens // BLK
    n_inner = lax.axis_size("inner")
    start_pos = (lax.axis_index("seq") * n_inner + lax.axis_index("inner")) * tokens
    seg_block = block_list // (n_inner * per_piece) * per_piece + block_list % per_piece
    seg_keys, seg_values = (
        lax.all_gather(keys, "seq", axis=0, tiled=True),
        lax.all_gather(values, "seq", axis=0, tiled=True),
    )
    key_blocks = seg_keys.reshape(-1, BLK, kv_loc, width)
    value_blocks = seg_values.reshape(-1, BLK, kv_loc, width)
    picked_keys = key_blocks[seg_block]
    picked_values = value_blocks[seg_block]
    lower = jnp.arange(SEL)[None, :] < jnp.arange(SEL)[:, None]
    repeat = jnp.any((block_list[:, :, None] == block_list[:, None, :]) & lower[None], axis=2)
    keep_all = jnp.logical_not(repeat)
    query_pos = start_pos + jnp.arange(tokens).reshape(per_piece, BLK)
    key_pos = block_list[:, :, None] * BLK + jnp.arange(BLK)[None, None, :]
    q_blocks = queries.reshape(per_piece, BLK, kv_loc, rep, width)

    def one_block(args):
        qblk, pk, pv, qpos, kpos, keep = args
        valid = keep[None, :, None] & (kpos[None] <= qpos[:, None, None])
        score = jnp.einsum(
            "qkrd,jukd->krqju", qblk, pk, preferred_element_type=jnp.float32
        ) * width ** (-0.5)
        score = jnp.where(valid[None, None], score, -1e30)
        top = jnp.max(score, axis=(3, 4), keepdims=True)
        expo = jnp.where(valid[None, None], jnp.exp(score - top), 0.0)
        denom = jnp.sum(expo, axis=(3, 4))
        weights = expo.astype(jnp.bfloat16)
        out = jnp.einsum("krqju,jukd->qkrd", weights, pv, preferred_element_type=jnp.float32)
        return out / jnp.transpose(denom, (2, 0, 1))[:, :, :, None]

    outs = lax.map(one_block, (q_blocks, picked_keys, picked_values, query_pos, key_pos, keep_all))
    sparse = outs.reshape(tokens, heads_loc, width)
    return (normed + sparse).astype(jnp.bfloat16)


def solution(mesh):
    return jax.shard_map(
        shards,
        mesh=mesh,
        in_specs=(
            P(("groups", "seq", "inner"), "head", None),
            P(("groups", "seq", "inner"), "head", None),
            P(("groups", "seq", "inner"), "head", None),
            P(("groups", "seq", "inner"), "head"),
            P("head", None),
            P(("groups", "seq", "inner"), None),
        ),
        out_specs=P(("groups", "seq", "inner"), "head", None),
        check_vma=False,
    )
```

profile of v0, /device:TPU:0, one launch (start us, length us, event | category | flops | bytes accessed | tf_op | source)
XLA Modules:
  0.0 109.6 jit_solution(16745564901405145584)
XLA Ops:
  6.5 0.8 copy.113
  7.3 0.2 reduce_window_sum.11
  7.5 0.6 slice_bitcast_fusion
  8.1 1.0 convert_multiply_fusion
  9.2 1.8 %fusion.30 = f32[2,128,128]{2,1,0:T(8,128)} fusion(f32[128,2,128]{2,1,0:T(2,128)S(1)} %convert_multiply_fusion, bf16[128,2,128]{2,1,0:T(2,128)(2,1)} %param.12), kind=kOutput, calls=%fused_computation.44 | convolution fusion | flops 50331648 | bytes 327680 | tf_op jit(solution)/shard_map/skd,ske->kde/dot_general | solution.py:47
  11.0 0.9 copy.121
  11.9 0.9 copy.129
  12.7 16.1 %all_gather.19 = bf16[512,2,128]{2,0,1:T(8,128)(2,1)S(1)} all-gather(bf16[128,2,128]{2,0,1:T(8,128)(2,1)S(1)} %copy.121), channel_id=1, replica_groups=mesh['groups'=2,'seq'=4,'inner'=2,'head'=2] {'seq'}, dimensions={0}, use_global_device_ids=true | all-gather | bytes 327680 | tf_op jit(solution)/shard_map/all_gather | solution.py:65
  28.8 0.7 broadcast_multiply_fusion
  29.6 0.9 and_reduce_fusion
  30.5 0.6 not.3
  31.2 0.6 add_add_fusion
  31.8 15.7 %all_gather.20 = bf16[512,2,128]{2,0,1:T(8,128)(2,1)S(1)} all-gather(bf16[128,2,128]{2,0,1:T(8,128)(2,1)S(1)} %copy.129), channel_id=1, replica_groups=mesh['groups'=2,'seq'=4,'inner'=2,'head'=2] {'seq'}, dimensions={0}, use_global_device_ids=true | all-gather | bytes 327680 | tf_op jit(solution)/shard_map/all_gather | solution.py:64
  47.5 0.7 gather_fusion
  48.2 0.9 gather_fusion.1
  49.2 18.8 %while.24 = (s32[]{:T(128)}, f32[2,64,2,8,128]{4,3,2,1,0:T(8,128)S(1)}, bf16[2,16,64,2,128]{4,2,3,1,0:T(8,128)(2,1)S(1)}, pred[2,16]{1,0:T(4,128)(4,1)}, s32[2,1...) while((s32[]{:T(128)}, ...), condition=%wide.region_8.9_spmd, body=%wide.region_5.8_spmd.sunk | while | flops 550762496 | bytes 18383788 | solution.py:92
  49.2 0.7 fusion.47
  49.9 0.7 fusion.48
  50.6 0.2 compare_and_fusion.2
  50.8 1.0 constant_dynamic-slice_fusion.7
  51.8 1.8 %fusion.49 = (f32[2,8,64]{2,1,0:T(8,128)S(1)}, f32[2,16,64,64,8]{3,2,4,1,0:T(8,128)S(1)}) fusion(pred[64,16,64]{0,2,1:T(8,128)(4,1)S(1)} %compare_and_fusion.2, bf16[1,64,2,8,128]{4,3,2,1,0:T(8,128)(2,1)S(1)} %constant_dynamic-slice_fusion.7, bf16[1,16,64,2,128]{4,2,3,1,0:T(8,128)(2,1)S(1)} %get-tuple-element.348), kind=kOutput, calls=%fused_computation.4.clone.1 | convolution fusion | flops 271580160 | bytes 5050368 | tf_op jit(solution)/shard_map/while/body/eval_jaxpr/qkrd,jukd->krqju/dot_general | solution.py:81
  53.6 2.3 %fusion.50 = f32[2,8,64]{2,1,0:T(8,128)S(1)} fusion(f32[2,16,64,64,8]{3,2,4,1,0:T(8,128)S(1)} %get-tuple-element.349, f32[2,8,64]{2,1,0:T(8,128)S(1)} %get-tuple-element.350, pred[64,16,64]{0,2,1:T(8,128)(4,1)S(1)} %compare_and_fusion.2), kind=kLoop, calls=%fused_computation.5.clone.1 | loop fusion | flops 5241856 | bytes 4268032 | tf_op jit(solution)/shard_map/while/body/eval_jaxpr/reduce_sum | solution.py:87
  55.9 2.3 %fusion.51 = f32[1,64,2,8,128]{4,1,3,2,0:T(8,128)S(1)} fusion(f32[2,16,64,64,8]{3,2,4,1,0:T(8,128)S(1)} %get-tuple-element.349, f32[2,8,64]{2,1,0:T(8,128)S(1)} %get-tuple-element.350, pred[64,16,64]{0,2,1:T(8,128)(4,1)S(1)} %compare_and_fusion.2, bf16[1,16,64,2,128]{4,2,3,1,0:T(8,128)(2,1)S(1)} %get-tuple-element.351, f32[64,2,8]{0,2,1:T(8,128)S(1)} %bitcast.148), kind=kOutput, calls=%fused_computation.11.clone.1 | convolution fusion | flops 273809408 | bytes 5316608 | tf_op jit(solution)/shard_map/while/body/eval_jaxpr/krqju,jukd->qkrd/dot_general | solution.py:89
  58.2 0.4 copy_dynamic-update-slice_fusion.2
  58.6 0.7 fusion.47
  59.3 0.7 fusion.48
  59.9 0.2 compare_and_fusion.2
  60.2 1.0 constant_dynamic-slice_fusion.7
  61.2 1.8 %fusion.49 = (f32[2,8,64]{2,1,0:T(8,128)S(1)}, f32[2,16,64,64,8]{3,2,4,1,0:T(8,128)S(1)}) fusion(pred[64,16,64]{0,2,1:T(8,128)(4,1)S(1)} %compare_and_fusion.2, bf16[1,64,2,8,128]{4,3,2,1,0:T(8,128)(2,1)S(1)} %constant_dynamic-slice_fusion.7, bf16[1,16,64,2,128]{4,2,3,1,0:T(8,128)(2,1)S(1)} %get-tuple-element.348), kind=kOutput, calls=%fused_computation.4.clone.1 | convolution fusion | flops 271580160 | bytes 5050368 | tf_op jit(solution)/shard_map/while/body/eval_jaxpr/qkrd,jukd->krqju/dot_general | solution.py:81
  63.0 2.3 %fusion.50 = f32[2,8,64]{2,1,0:T(8,128)S(1)} fusion(f32[2,16,64,64,8]{3,2,4,1,0:T(8,128)S(1)} %get-tuple-element.349, f32[2,8,64]{2,1,0:T(8,128)S(1)} %get-tuple-element.350, pred[64,16,64]{0,2,1:T(8,128)(4,1)S(1)} %compare_and_fusion.2), kind=kLoop, calls=%fused_computation.5.clone.1 | loop fusion | flops 5241856 | bytes 4268032 | tf_op jit(solution)/shard_map/while/body/eval_jaxpr/reduce_sum | solution.py:87
  65.3 2.3 %fusion.51 = f32[1,64,2,8,128]{4,1,3,2,0:T(8,128)S(1)} fusion(f32[2,16,64,64,8]{3,2,4,1,0:T(8,128)S(1)} %get-tuple-element.349, f32[2,8,64]{2,1,0:T(8,128)S(1)} %get-tuple-element.350, pred[64,16,64]{0,2,1:T(8,128)(4,1)S(1)} %compare_and_fusion.2, bf16[1,16,64,2,128]{4,2,3,1,0:T(8,128)(2,1)S(1)} %get-tuple-element.351, f32[64,2,8]{0,2,1:T(8,128)S(1)} %bitcast.148), kind=kOutput, calls=%fused_computation.11.clone.1 | convolution fusion | flops 273809408 | bytes 5316608 | tf_op jit(solution)/shard_map/while/body/eval_jaxpr/krqju,jukd->qkrd/dot_general | solution.py:89
  67.6 0.4 copy_dynamic-update-slice_fusion.2
  68.0 20.6 %all-gather.1 = f32[8,1,2]{2,1,0:T(1,128)S(1)} all-gather(f32[1,1,2]{2,1,0:T(1,128)S(1)} %copy-done.4), channel_id=1, replica_groups=mesh['groups'=2,'seq'=4,'inner'=2,'head'=2] {'seq','inner'}, dimensions={0}, use_global_device_ids=true | all-gather | bytes 72 | tf_op jit(solution)/shard_map/all_gather | solution.py:13
  88.7 0.1 exponential_select_fusion.1
  88.9 1.4 %fusion.26 = f32[2,8,128,128]{2,3,1,0:T(8,128)S(1)} fusion(f32[2,128,128]{1,2,0:T(8,128)S(1)} %exponential_select_fusion.1, bf16[128,2,8,128]{3,2,1,0:T(8,128)(2,1)} %bitcast.138, bf16[128,2,128,1]{2,1,0,3:T(2,128)(2,1)S(1)} %bitcast.144), kind=kOutput, calls=%fused_computation.38 | convolution fusion | flops 67371008 | bytes 1769472 | tf_op jit(solution)/shard_map/tkrd,skd->krts/dot_general | solution.py:42
  90.2 0.7 convolution_bitcast_fusion.2
  91.0 8.3 %while.25 = (s32[]{:T(128)}, f32[2,128,128]{2,1,0:T(8,128)S(1)}, s32[]{:T(128)}, f32[8,2]{1,0:T(8,128)S(1)}, f32[8,2,128,128]{3,2,1,0:T(8,128)}, /*index=5*/s32[]{:T(128)}, s32[]{:T(128)}) while((s32[]{:T(128)}, f32[2,128,128]{2,1,0:T(8,128)S(1)}, s32[]{:T(128)}, f32[8,2]{1,0:T(8,128)S(1)}, f32[8,2,128,128]{3,2,1,0:T(8,128)}, ...), condition=%wide.region_2.3_spmd.clone, body=%wide.region_1.2_spmd.clone.sunk | while | flops 131076 | bytes 393353 | solution.py:25
  91.0 1.0 fusion.52
  92.0 1.0 fusion.52
  93.1 1.0 fusion.52
  94.1 1.0 fusion.52
  95.1 1.0 fusion.52
  96.2 1.0 fusion.52
  97.2 1.0 fusion.52
  98.2 1.0 fusion.52
  99.2 1.8 %multiply_reduce_fusion = (f32[128,2,8]{0,2,1:T(8,128)S(1)}, f32[128,2,8,128]{0,3,2,1:T(8,128)S(1)}) fusion(f32[128,2,8,128]{0,3,2,1:T(8,128)S(1)} %convolution_bitcast_fusion.2, bf16[128,2,8,128]{3,2,1,0:T(8,128)(2,1)} %bitcast.139, f32[2,128,128]{2,1,0:T(8,128)S(1)} %get-tuple-element.141, f32[128,2]{0,1:T(2,128)S(1)} %copy.118), kind=kOutput, calls=%fused_computation.40 | convolution fusion | flops 403699712 | bytes 2761728 | tf_op jit(solution)/shard_map/tkrd,kde->tkre/dot_general | solution.py:52
  101.0 0.5 copy.126
  101.6 1.1 %add_convert_fusion = bf16[128,16,128]{2,1,0:T(8,128)(2,1)} fusion(f32[128,16,128]{2,1,0:T(8,128)S(1)} %bitcast.143, f32[128,16,128]{2,1,0:T(8,128)S(1)} %copy.126, f32[16,128]{1,0:T(8,128)S(1)} %copy-done.3, f32[128,16]{1,0:T(8,128)S(1)} %copy.125), kind=kLoop, calls=%fused_computation.39 | loop fusion | flops 1048576 | bytes 2637824 | tf_op jit(solution)/shard_map/convert_element_type | solution.py:94
  (39 shorter events, 0.8 us)
Async XLA Ops:
  6.5 84.4 %all-gather.4.cloned.1.call-start = ((), (), s32[]{:S(2)}) async-start(), calls=%async_computation | async-start | bytes 1179648 | tf_op jit(solution)/shard_map/all_gather | solution.py:13
  29.6 17.9 %copy-start.2 = (s32[1024]{0:T(1024)}, s32[1024]{0:T(1024)S(1)}, u32[]{:S(2)}) copy-start(s32[1024]{0:T(1024)S(1)} %pad_clamp_fusion) | copy-start | bytes 12292
  49.1 18.8 %copy-start.4 = (f32[1,1,2]{2,1,0:T(1,128)S(1)}, f32[1,1,2]{2,1,0:T(1,128)}, u32[]{:S(2)}) copy-start(f32[1,1,2]{2,1,0:T(1,128)} %get-tuple-element.264) | copy-start | bytes 28
  49.1 39.7 %copy-start = (bf16[128,2,128]{2,1,0:T(2,128)(2,1)S(1)}, bf16[128,2,128]{2,1,0:T(2,128)(2,1)}, u32[]{:S(2)}) copy-start(bf16[128,2,128]{2,1,0:T(2,128)(2,1)} %param.11) | copy-start | bytes 196612
  49.2 41.1 %copy-start.1 = (bf16[128,2,128]{2,1,0:T(2,128)(2,1)S(1)}, bf16[128,2,128]{2,1,0:T(2,128)(2,1)}, u32[]{:S(2)}) copy-start(bf16[128,2,128]{2,1,0:T(2,128)(2,1)} %param.12) | copy-start | bytes 196612
  67.9 33.7 %copy-start.3 = (f32[16,128]{1,0:T(8,128)S(1)}, f32[16,128]{1,0:T(8,128)}, u32[]{:S(2)}) copy-start(f32[16,128]{1,0:T(8,128)} %param.14) | copy-start | bytes 24580
Sparse Core Ops, SparseCore 0:
  11.1 43.3 all-gather.3
where the time goes:
time: 110 us
  blocking collectives  52.4 us (48%)
  other arithmetic  18.3 us (17%)
  matrix products  13.7 us (12%)
  between operations  13.6 us (12%)
  local copies, waits for them, and re-layouts  11.2 us (10%)
    all_gather x1, blocking collectives, prefix(): everything = jax.tree.map(lambda part: lax.all_gather(part, axis), shard)  20.6 us
    all_gather x1, blocking collectives, shards(): lax.all_gather(values, 'seq', axis=0, tiled=True)  16.1 us
    all_gather x1, blocking collectives, shards(): lax.all_gather(keys, 'seq', axis=0, tiled=True)  15.7 us
    select_n x8, other arithmetic, turn(): return jax.tree.map(lambda a, b: jnp.where(reached, a, b), new, before)  7.94 us
    dot_general x2, matrix products, one_block(): jnp.einsum('krqju,jukd->qkrd', weights, pv, preferred_element_type=jnp.fl...  4.6 us
    reduce_sum x2, other arithmetic, one_block(): denom = jnp.sum(expo, axis=(3, 4))  4.54 us
    dot_general x2, matrix products, one_block(): jnp.einsum('qkrd,jukd->krqju', qblk, pk, preferred_element_type=jnp.float32)  3.54 us
    unnamed x13, local copies, waits for them, and re-layouts  2.52 us
  transfers between devices with their start and end apart: 1, of which 0 were waited for; matrix products, arithmetic and copies ran while one was open for 25% of the time, Pallas kernels for 0%

commit v1 on v0

--- a/solution.py
+++ b/solution.py
@@ -6,6 +6,24 @@
 BLK = 64
 SEL = 16
 HIGH = lax.Precision.HIGHEST
+
+
+def _wrap_quotas(m, along_dim):
+    r1 = list(m.shape[1:])
+    r1[along_dim] *= m.shape[0]
+    return jnp.moveaxis(m, 0, along_dim).reshape(r1)
+
+
+def press_cube(xin, chip_axis):
+    far_arr = xin[None]
+    n_shards = lax.psum(1, axis_name=chip_axis)
+    for nth in range(n_shards.bit_length() - 1):
+        local_out = 1 << nth
+        w2 = lax.ppermute(far_arr, chip_axis, tuple(((p, p ^ local_out) for p in range(n_shards))))
+        res = jnp.stack([far_arr, w2], axis=0)
+        fresh = lax.axis_index(chip_axis) >> nth & 1
+        far_arr = jnp.where(fresh == 0, res, res[::-1]).reshape(-1, *xin.shape)
+    return far_arr
 
 
 def prefix(shard, axis, combine, identity):
@@ -60,8 +78,12 @@
     n_inner = lax.axis_size("inner")
     start_pos = (lax.axis_index("seq") * n_inner + lax.axis_index("inner")) * tokens
     seg_block = block_list // (n_inner * per_piece) * per_piece + block_list % per_piece
+
+    def bands_solve(incoming_x, tile_in, array_axis):
+        return _wrap_quotas(press_cube(incoming_x, tile_in), array_axis)
+
     seg_keys, seg_values = (
-        lax.all_gather(keys, "seq", axis=0, tiled=True),
+        bands_solve(keys, "seq", 0),
         lax.all_gather(values, "seq", axis=0, tiled=True),
     )
     key_blocks = seg_keys.reshape(-1, BLK, kv_loc, width)

time: 110 us -> 98.3 us (0.89)
  blocking collectives: 52.4 us -> 36.2 us
  starting transfers between devices: 0.01 us -> 5.78 us
  local copies, waits for them, and re-layouts: 11.2 us -> 7.46 us
  matrix products: 13.7 us -> 15.7 us
    all_gather x1 -> x0, blocking collectives: 15.7 us -> none  [shards(): lax.all_gather(keys, 'seq', axis=0, tiled=True)]
    ppermute x0 -> x2, starting transfers between devices: none -> 5.78 us  [press_cube(): lax.ppermute(far_arr, chip_axis, tuple(((p, p ^ local_out) for p in range...]
    all_gather x1, blocking collectives: 20.6 us -> 17.9 us  [prefix(): everything = jax.tree.map(lambda part: lax.all_gather(part, axis), shard)]
    all_gather x1, blocking collectives: 16.1 us -> 18.3 us  [shards(): lax.all_gather(values, 'seq', axis=0, tiled=True)]
    dynamic_slice x4, local copies, waits for them, and re-layouts: 2.11 us -> 0.21 us  [shards(): lax.map(one_block, (q_blocks, picked_keys, picked_values, query_pos, key_...]
    dot_general x1, matrix products: 0.68 us -> 2.5 us  [shards(): jnp.einsum('krts,skd->tkrd', scores * weight[:, None], vf, precision=HIGH)]
    dynamic_update_slice x2, local copies, waits for them, and re-layouts: 0.7 us -> 2.22 us  [shards(): lax.map(one_block, (q_blocks, picked_keys, picked_values, query_pos, key_...]
    le x4, local copies, waits for them, and re-layouts: 1.38 us -> 0.02 us  [one_block(): valid = keep[None, :, None] & (kpos[None] <= qpos[:, None, None])]
  transfers between devices with their start and end apart: 1 -> 3, of which waited for: 0 -> 0; matrix products, arithmetic and copies ran while one was open for 25% -> 29% of each run, Pallas kernels for 0% -> 0%
where the time goes in v1:
time: 98.3 us; the launch traced here: 97.6 us
  blocking collectives  36.2 us (37%)
  other arithmetic  18.5 us (19%)
  matrix products  15.7 us (16%)
  between operations  13.6 us (14%)
  local copies, waits for them, and re-layouts  7.46 us (8%)
  starting transfers between devices  5.78 us (6%)
    all_gather x1, blocking collectives, shards(): lax.all_gather(values, 'seq', axis=0, tiled=True)  18.3 us
    all_gather x1, blocking collectives, prefix(): everything = jax.tree.map(lambda part: lax.all_gather(part, axis), shard)  17.9 us
    select_n x8, other arithmetic, turn(): return jax.tree.map(lambda a, b: jnp.where(reached, a, b), new, before)  7.94 us
    ppermute x2, starting transfers between devices, press_cube(): lax.ppermute(far_arr, chip_axis, tuple(((p, p ^ local_out) for p in range...  5.78 us
    dot_general x2, matrix products, one_block(): jnp.einsum('krqju,jukd->qkrd', weights, pv, preferred_element_type=jnp.fl...  4.55 us
    reduce_sum x2, other arithmetic, one_block(): denom = jnp.sum(expo, axis=(3, 4))  4.53 us
    dot_general x2, matrix products, one_block(): jnp.einsum('qkrd,jukd->krqju', qblk, pk, preferred_element_type=jnp.float32)  3.55 us
    unnamed x7, local copies, waits for them, and re-layouts  2.55 us
  transfers between devices with their start and end apart: 3, of which 0 were waited for; matrix products, arithmetic and copies ran while one was open for 29% of the time, Pallas kernels for 0%

profile of v1, /device:TPU:0, one launch (start us, length us, event | category | flops | bytes accessed | tf_op | source)
XLA Modules:
  0.0 97.6 jit_solution(6217585853941498282)
XLA Ops:
  6.5 0.9 copy.194
  7.4 3.1 %collective-permute-start = (bf16[1,128,2,128]{3,1,2,0:T(8,128)(2,1)S(1)}, bf16[1,128,2,128]{3,1,2,0:T(8,128)(2,1)S(1)}, u32[]{:S(2)}, u32[]{:S(2)}) collective-permute-start(bf16[1,128,2,128]{3,1,2,0:T(8,128)(2,1)S(1)} %bitcast.160), channel_id=1, source_target_pairs={{0,4},{4,0},{8,12},{12,8},{1,5},{5,1},{9,13},{13,9},{2,6},{6,2},{1... | collective-permute-start | bytes 196616 | tf_op jit(solution)/shard_map/ppermute | solution.py:22
  10.6 0.8 copy.117
  11.4 0.2 reduce_window_sum.11
  11.6 1.0 %convert_multiply_fusion = f32[128,2,128]{2,1,0:T(2,128)S(1)} fusion(bf16[128,2,128]{2,1,0:T(2,128)(2,1)} %param.11, f32[128,2]{1,0:T(8,128)S(1)} %get-tuple-element.263), kind=kLoop, calls=%fused_computation.50 | loop fusion | flops 65536 | bytes 197632 | tf_op jit(solution)/shard_map/mul | solution.py:65
  12.6 1.8 %fusion.30 = f32[2,128,128]{2,1,0:T(8,128)} fusion(f32[128,2,128]{2,1,0:T(2,128)S(1)} %convert_multiply_fusion, bf16[128,2,128]{2,1,0:T(2,128)(2,1)} %param.12), kind=kOutput, calls=%fused_computation.48 | convolution fusion | flops 50331648 | bytes 327680 | tf_op jit(solution)/shard_map/skd,ske->kde/dot_general | solution.py:65
  14.4 0.9 copy.125
  15.3 0.7 broadcast_multiply_fusion
  16.0 0.1 reshape.119
  16.1 0.1 iota_add_fusion
  16.2 0.9 and_reduce_fusion
  17.1 0.1 copy.118
  17.2 0.1 exponential_select_fusion.1
  17.3 1.4 %fusion.26 = f32[2,8,128,128]{2,3,1,0:T(8,128)S(1)} fusion(f32[2,128,128]{1,2,0:T(8,128)S(1)} %exponential_select_fusion.1, bf16[128,2,8,128]{3,2,1,0:T(8,128)(2,1)} %bitcast.150, bf16[128,2,128,1]{2,1,0,3:T(2,128)(2,1)} %bitcast.156), kind=kOutput, calls=%fused_computation.38 | convolution fusion | flops 67371008 | bytes 1769472 | tf_op jit(solution)/shard_map/tkrd,skd->krts/dot_general | solution.py:60
  18.7 2.5 %convolution_bitcast_fusion.2 = f32[128,2,8,128]{0,3,2,1:T(8,128)} fusion(f32[2,8,128,128]{2,3,1,0:T(8,128)S(1)} %fusion.26, bf16[128,2,128,1]{2,1,0,3:T(2,128)(2,1)} %bitcast.157), kind=kOutput, calls=%fused_computation.37 | convolution fusion | flops 402653184 | bytes 2162688 | tf_op jit(solution)/shard_map/krts,skd->tkrd/dot_general | solution.py:63
  21.3 2.7 %collective-permute-start.1 = (bf16[2,128,2,128]{3,1,0,2:T(8,128)(2,1)S(1)}, bf16[2,128,2,128]{3,1,0,2:T(8,128)(2,1)S(1)}, u32[]{:S(2)}, u32[]{:S(2)}) collective-permute-start(bf16[2,128,2,128]{3,1,0,2:T(8,128)(2,1)S(1)} %get-tuple-element.262), channel_id=1, source_target_pairs={{0,8},{4,12},{8,0},{12,4},{1,9},{5,13},{9,1},{13,5},{2,10},{6,14},... | collective-permute-start | bytes 393224 | tf_op jit(solution)/shard_map/ppermute | solution.py:22
  24.0 18.3 %all_gather.16 = bf16[512,2,128]{2,0,1:T(8,128)(2,1)S(1)} all-gather(bf16[128,2,128]{2,0,1:T(8,128)(2,1)S(1)} %copy.125), channel_id=1, replica_groups=mesh['groups'=2,'seq'=4,'inner'=2,'head'=2] {'seq'}, dimensions={0}, use_global_device_ids=true | all-gather | bytes 327680 | tf_op jit(solution)/shard_map/all_gather | solution.py:87
  42.2 17.9 %all-gather.1 = f32[8,1,2]{2,1,0:T(1,128)S(1)} all-gather(f32[1,1,2]{2,1,0:T(1,128)S(1)} %get-tuple-element.266), channel_id=1, replica_groups=mesh['groups'=2,'seq'=4,'inner'=2,'head'=2] {'seq','inner'}, dimensions={0}, use_global_device_ids=true | all-gather | bytes 72 | tf_op jit(solution)/shard_map/all_gather | solution.py:31
  60.2 0.1 copy.122
  60.2 0.8 gather_fusion
  61.1 0.1 reverse_select_fusion
  61.2 0.7 gather_fusion.1
  61.9 15.7 %while.24 = (s32[]{:T(128)}, f32[2,64,2,8,128]{4,3,2,1,0:T(8,128)}, bf16[2,16,64,2,128]{4,2,3,1,0:T(8,128)(2,1)S(1)}, pred[2,16]{1,0:T(4,128)(4,1)S(1)}, s32[2,1...) while((s32[]{:T(128)}, f32[2,64,2,8,128]{4,3,2,1,0:T(8,128)}, ...), condition=%wide.region_8.9_spmd, body=%wide.region_5.8_spmd.sunk | while | flops 550762496 | bytes 18384288 | solution.py:114
  62.0 0.2 compare_and_fusion.2
  62.2 0.1 constant_dynamic-slice_fusion.8
  62.3 1.8 %fusion.51 = (f32[2,8,64]{2,1,0:T(8,128)S(1)}, f32[2,16,64,64,8]{3,2,4,1,0:T(8,128)S(1)}) fusion(pred[64,16,64]{0,2,1:T(8,128)(4,1)S(1)} %compare_and_fusion.2, bf16[1,64,2,8,128]{4,3,2,1,0:T(8,128)(2,1)S(1)} %constant_dynamic-slice_fusion.7, bf16[1,16,64,2,128]{4,2,3,1,0:T(8,128)(2,1)S(1)} %get-tuple-element.352), kind=kOutput, calls=%fused_computation.4.clone.1 | convolution fusion | flops 271580160 | bytes 5050368 | tf_op jit(solution)/shard_map/while/body/eval_jaxpr/qkrd,jukd->krqju/dot_general | solution.py:103
  64.1 2.3 %fusion.52 = f32[2,8,64]{2,1,0:T(8,128)S(1)} fusion(f32[2,16,64,64,8]{3,2,4,1,0:T(8,128)S(1)} %get-tuple-element.353, f32[2,8,64]{2,1,0:T(8,128)S(1)} %get-tuple-element.354, pred[64,16,64]{0,2,1:T(8,128)(4,1)S(1)} %compare_and_fusion.2), kind=kLoop, calls=%fused_computation.5.clone.1 | loop fusion | flops 5241856 | bytes 4268032 | tf_op jit(solution)/shard_map/while/body/eval_jaxpr/reduce_sum | solution.py:109
  66.4 2.3 %fusion.53 = f32[1,64,2,8,128]{4,1,3,2,0:T(8,128)S(1)} fusion(f32[2,16,64,64,8]{3,2,4,1,0:T(8,128)S(1)} %get-tuple-element.353, f32[2,8,64]{2,1,0:T(8,128)S(1)} %get-tuple-element.354, pred[64,16,64]{0,2,1:T(8,128)(4,1)S(1)} %compare_and_fusion.2, bf16[1,16,64,2,128]{4,2,3,1,0:T(8,128)(2,1)S(1)} %get-tuple-element.355, f32[64,2,8]{0,2,1:T(8,128)S(1)} %bitcast.162), kind=kOutput, calls=%fused_computation.11.clone.1 | convolution fusion | flops 273809408 | bytes 5316608 | tf_op jit(solution)/shard_map/while/body/eval_jaxpr/krqju,jukd->qkrd/dot_general | solution.py:111
  68.7 1.1 %copy_dynamic-update-slice_fusion.2 = f32[2,64,2,8,128]{4,3,2,1,0:T(8,128)} fusion(f32[2,64,2,8,128]{4,3,2,1,0:T(8,128)} %get-tuple-element.371, s32[]{:T(128)} %get-tuple-element.370, f32[1,64,2,8,128]{4,1,3,2,0:T(8,128)S(1)} %fusion.53), kind=kLoop, calls=%fused_computation.13.clone.1 | loop fusion | bytes 1049088 | tf_op jit(solution)/shard_map/while/body/jit(dynamic_update_index_in_dim)/dynamic_update_slice | solution.py:114
  69.8 0.2 compare_and_fusion.2
  70.0 0.1 constant_dynamic-slice_fusion.8
  70.2 1.8 %fusion.51 = (f32[2,8,64]{2,1,0:T(8,128)S(1)}, f32[2,16,64,64,8]{3,2,4,1,0:T(8,128)S(1)}) fusion(pred[64,16,64]{0,2,1:T(8,128)(4,1)S(1)} %compare_and_fusion.2, bf16[1,64,2,8,128]{4,3,2,1,0:T(8,128)(2,1)S(1)} %constant_dynamic-slice_fusion.7, bf16[1,16,64,2,128]{4,2,3,1,0:T(8,128)(2,1)S(1)} %get-tuple-element.352), kind=kOutput, calls=%fused_computation.4.clone.1 | convolution fusion | flops 271580160 | bytes 5050368 | tf_op jit(solution)/shard_map/while/body/eval_jaxpr/qkrd,jukd->krqju/dot_general | solution.py:103
  71.9 2.3 %fusion.52 = f32[2,8,64]{2,1,0:T(8,128)S(1)} fusion(f32[2,16,64,64,8]{3,2,4,1,0:T(8,128)S(1)} %get-tuple-element.353, f32[2,8,64]{2,1,0:T(8,128)S(1)} %get-tuple-element.354, pred[64,16,64]{0,2,1:T(8,128)(4,1)S(1)} %compare_and_fusion.2), kind=kLoop, calls=%fused_computation.5.clone.1 | loop fusion | flops 5241856 | bytes 4268032 | tf_op jit(solution)/shard_map/while/body/eval_jaxpr/reduce_sum | solution.py:109
  74.2 2.3 %fusion.53 = f32[1,64,2,8,128]{4,1,3,2,0:T(8,128)S(1)} fusion(f32[2,16,64,64,8]{3,2,4,1,0:T(8,128)S(1)} %get-tuple-element.353, f32[2,8,64]{2,1,0:T(8,128)S(1)} %get-tuple-element.354, pred[64,16,64]{0,2,1:T(8,128)(4,1)S(1)} %compare_and_fusion.2, bf16[1,16,64,2,128]{4,2,3,1,0:T(8,128)(2,1)S(1)} %get-tuple-element.355, f32[64,2,8]{0,2,1:T(8,128)S(1)} %bitcast.162), kind=kOutput, calls=%fused_computation.11.clone.1 | convolution fusion | flops 273809408 | bytes 5316608 | tf_op jit(solution)/shard_map/while/body/eval_jaxpr/krqju,jukd->qkrd/dot_general | solution.py:111
  76.5 1.1 %copy_dynamic-update-slice_fusion.2 = f32[2,64,2,8,128]{4,3,2,1,0:T(8,128)} fusion(f32[2,64,2,8,128]{4,3,2,1,0:T(8,128)} %get-tuple-element.371, s32[]{:T(128)} %get-tuple-element.370, f32[1,64,2,8,128]{4,1,3,2,0:T(8,128)S(1)} %fusion.53), kind=kLoop, calls=%fused_computation.13.clone.1 | loop fusion | bytes 1049088 | tf_op jit(solution)/shard_map/while/body/jit(dynamic_update_index_in_dim)/dynamic_update_slice | solution.py:114
  77.6 8.2 %while.25 = (s32[]{:T(128)}, f32[2,128,128]{2,1,0:T(8,128)S(1)}, s32[]{:T(128)}, f32[8,2]{1,0:T(8,128)S(1)}, f32[8,2,128,128]{3,2,1,0:T(8,128)}, /*index=5*/s32[]{:T(128)}, s32[]{:T(128)}) while((s32[]{:T(128)}, f32[2,128,128]{2,1,0:T(8,128)S(1)}, s32[]{:T(128)}, f32[8,2]{1,0:T(8,128)S(1)}, f32[8,2,128,128]{3,2,1,0:T(8,128)}, ...), condition=%wide.region_2.3_spmd.clone, body=%wide.region_1.2_spmd.clone.sunk | while | flops 131076 | bytes 393345 | solution.py:43
  77.6 1.0 %fusion.54 = f32[2,128,128]{2,1,0:T(8,128)S(1)} fusion(f32[8,2,128,128]{3,2,1,0:T(8,128)} %get-tuple-element.406, s32[]{:T(128)} %get-tuple-element.395, f32[2,128,128]{2,1,0:T(8,128)S(1)} %get-tuple-element.396, f32[2]{0:T(128)S(1)} %dynamic-slice_bitcast_fusion.5, pred[]{:T(512)S(6)} %compare.6, pred[]{:T(512)S(6)} %lt.67), kind=kLoop, calls=%fused_computation.31.clone.1 | loop fusion | flops 131072 | bytes 393230 | tf_op jit(solution)/shard_map/while/body/eval_jaxpr/jit(_where)/select_n | solution.py:41
  78.7 1.0 %fusion.54 = f32[2,128,128]{2,1,0:T(8,128)S(1)} fusion(f32[8,2,128,128]{3,2,1,0:T(8,128)} %get-tuple-element.406, s32[]{:T(128)} %get-tuple-element.395, f32[2,128,128]{2,1,0:T(8,128)S(1)} %get-tuple-element.396, f32[2]{0:T(128)S(1)} %dynamic-slice_bitcast_fusion.5, pred[]{:T(512)S(6)} %compare.6, pred[]{:T(512)S(6)} %lt.67), kind=kLoop, calls=%fused_computation.31.clone.1 | loop fusion | flops 131072 | bytes 393230 | tf_op jit(solution)/shard_map/while/body/eval_jaxpr/jit(_where)/select_n | solution.py:41
  79.7 1.0 %fusion.54 = f32[2,128,128]{2,1,0:T(8,128)S(1)} fusion(f32[8,2,128,128]{3,2,1,0:T(8,128)} %get-tuple-element.406, s32[]{:T(128)} %get-tuple-element.395, f32[2,128,128]{2,1,0:T(8,128)S(1)} %get-tuple-element.396, f32[2]{0:T(128)S(1)} %dynamic-slice_bitcast_fusion.5, pred[]{:T(512)S(6)} %compare.6, pred[]{:T(512)S(6)} %lt.67), kind=kLoop, calls=%fused_computation.31.clone.1 | loop fusion | flops 131072 | bytes 393230 | tf_op jit(solution)/shard_map/while/body/eval_jaxpr/jit(_where)/select_n | solution.py:41
  80.7 1.0 %fusion.54 = f32[2,128,128]{2,1,0:T(8,128)S(1)} fusion(f32[8,2,128,128]{3,2,1,0:T(8,128)} %get-tuple-element.406, s32[]{:T(128)} %get-tuple-element.395, f32[2,128,128]{2,1,0:T(8,128)S(1)} %get-tuple-element.396, f32[2]{0:T(128)S(1)} %dynamic-slice_bitcast_fusion.5, pred[]{:T(512)S(6)} %compare.6, pred[]{:T(512)S(6)} %lt.67), kind=kLoop, calls=%fused_computation.31.clone.1 | loop fusion | flops 131072 | bytes 393230 | tf_op jit(solution)/shard_map/while/body/eval_jaxpr/jit(_where)/select_n | solution.py:41
  81.8 1.0 %fusion.54 = f32[2,128,128]{2,1,0:T(8,128)S(1)} fusion(f32[8,2,128,128]{3,2,1,0:T(8,128)} %get-tuple-element.406, s32[]{:T(128)} %get-tuple-element.395, f32[2,128,128]{2,1,0:T(8,128)S(1)} %get-tuple-element.396, f32[2]{0:T(128)S(1)} %dynamic-slice_bitcast_fusion.5, pred[]{:T(512)S(6)} %compare.6, pred[]{:T(512)S(6)} %lt.67), kind=kLoop, calls=%fused_computation.31.clone.1 | loop fusion | flops 131072 | bytes 393230 | tf_op jit(solution)/shard_map/while/body/eval_jaxpr/jit(_where)/select_n | solution.py:41
  82.8 1.0 %fusion.54 = f32[2,128,128]{2,1,0:T(8,128)S(1)} fusion(f32[8,2,128,128]{3,2,1,0:T(8,128)} %get-tuple-element.406, s32[]{:T(128)} %get-tuple-element.395, f32[2,128,128]{2,1,0:T(8,128)S(1)} %get-tuple-element.396, f32[2]{0:T(128)S(1)} %dynamic-slice_bitcast_fusion.5, pred[]{:T(512)S(6)} %compare.6, pred[]{:T(512)S(6)} %lt.67), kind=kLoop, calls=%fused_computation.31.clone.1 | loop fusion | flops 131072 | bytes 393230 | tf_op jit(solution)/shard_map/while/body/eval_jaxpr/jit(_where)/select_n | solution.py:41
  83.8 1.0 %fusion.54 = f32[2,128,128]{2,1,0:T(8,128)S(1)} fusion(f32[8,2,128,128]{3,2,1,0:T(8,128)} %get-tuple-element.406, s32[]{:T(128)} %get-tuple-element.395, f32[2,128,128]{2,1,0:T(8,128)S(1)} %get-tuple-element.396, f32[2]{0:T(128)S(1)} %dynamic-slice_bitcast_fusion.5, pred[]{:T(512)S(6)} %compare.6, pred[]{:T(512)S(6)} %lt.67), kind=kLoop, calls=%fused_computation.31.clone.1 | loop fusion | flops 131072 | bytes 393230 | tf_op jit(solution)/shard_map/while/body/eval_jaxpr/jit(_where)/select_n | solution.py:41
  84.8 1.0 %fusion.54 = f32[2,128,128]{2,1,0:T(8,128)S(1)} fusion(f32[8,2,128,128]{3,2,1,0:T(8,128)} %get-tuple-element.406, s32[]{:T(128)} %get-tuple-element.395, f32[2,128,128]{2,1,0:T(8,128)S(1)} %get-tuple-element.396, f32[2]{0:T(128)S(1)} %dynamic-slice_bitcast_fusion.5, pred[]{:T(512)S(6)} %compare.6, pred[]{:T(512)S(6)} %lt.67), kind=kLoop, calls=%fused_computation.31.clone.1 | loop fusion | flops 131072 | bytes 393230 | tf_op jit(solution)/shard_map/while/body/eval_jaxpr/jit(_where)/select_n | solution.py:41
  85.8 1.9 %multiply_reduce_fusion = (f32[128,2,8]{0,2,1:T(8,128)S(1)}, f32[128,2,8,128]{0,3,2,1:T(8,128)S(1)}) fusion(f32[128,2,8,128]{0,3,2,1:T(8,128)} %convolution_bitcast_fusion.2, bf16[128,2,8,128]{3,2,1,0:T(8,128)(2,1)S(1)} %bitcast.152, f32[2,128,128]{2,1,0:T(8,128)S(1)} %get-tuple-element.141, f32[128,2]{0,1:T(2,128)S(1)} %copy.122), kind=kOutput, calls=%fused_computation.40 | convolution fusion | flops 403699712 | bytes 2761728 | tf_op jit(solution)/shard_map/tkrd,kde->tkre/dot_general | solution.py:70
  87.8 0.5 copy.130
  88.3 0.1 copy.129
  88.4 2.4 %add_convert_fusion = bf16[128,16,128]{2,1,0:T(8,128)(2,1)} fusion(f32[128,16,128]{2,1,0:T(8,128)} %bitcast.45, f32[128,16,128]{2,1,0:T(8,128)S(1)} %copy.130, f32[16,128]{1,0:T(8,128)S(1)} %copy-done.1, f32[128,16]{1,0:T(8,128)S(1)} %copy.129), kind=kLoop, calls=%fused_computation.39 | loop fusion | flops 1048576 | bytes 2637824 | tf_op jit(solution)/shard_map/convert_element_type | solution.py:116
  (40 shorter events, 0.4 us)
Async XLA Ops:
  6.5 55.4 %copy-start = (bf16[128,16,128]{2,1,0:T(8,128)(2,1)S(1)}, bf16[128,16,128]{2,1,0:T(8,128)(2,1)}, u32[]{:S(2)}) copy-start(bf16[128,16,128]{2,1,0:T(8,128)(2,1)} %param.10) | copy-start | bytes 1572868
  6.5 71.1 %all-gather.4.cloned.1.call-start = ((), (), s32[]{:S(2)}) async-start(), calls=%async_computation | async-start | bytes 1179648 | tf_op jit(solution)/shard_map/all_gather | solution.py:31
  7.4 13.8 %collective-permute-start = (bf16[1,128,2,128]{3,1,2,0:T(8,128)(2,1)S(1)}, bf16[1,128,2,128]{3,1,2,0:T(8,128)(2,1)S(1)}, u32[]{:S(2)}, u32[]{:S(2)}) collective-permute-start(bf16[1,128,2,128]{3,1,2,0:T(8,128)(2,1)S(1)} %bitcast.160), channel_id=1, source_target_pairs={{0,4},{4,0},{8,12},{12,8},{1,5},{5,1},{9,13},{13,9},{2,6},{6,2},{1... | collective-permute-start | bytes 196616 | tf_op jit(solution)/shard_map/ppermute | solution.py:22
  21.3 39.7 %collective-permute-start.1 = (bf16[2,128,2,128]{3,1,0,2:T(8,128)(2,1)S(1)}, bf16[2,128,2,128]{3,1,0,2:T(8,128)(2,1)S(1)}, u32[]{:S(2)}, u32[]{:S(2)}) collective-permute-start(bf16[2,128,2,128]{3,1,0,2:T(8,128)(2,1)S(1)} %get-tuple-element.262), channel_id=1, source_target_pairs={{0,8},{4,12},{8,0},{12,4},{1,9},{5,13},{9,1},{13,5},{2,10},{6,14},... | collective-permute-start | bytes 393224 | tf_op jit(solution)/shard_map/ppermute | solution.py:22
  61.9 26.5 %copy-start.1 = (f32[16,128]{1,0:T(8,128)S(1)}, f32[16,128]{1,0:T(8,128)}, u32[]{:S(2)}) copy-start(f32[16,128]{1,0:T(8,128)} %param.14) | copy-start | bytes 24580
Sparse Core Ops, SparseCore 0:
  14.5 44.4 all-gather.3
